TPU v7x, 32 devices: a whole 2x2x4 slice. The times are simulated.
32 devices in a mesh: dom: 8 (over z, y), rep: 4 (over x, core).
Axes of the slice: x: 2, y: 2, z: 4, core: 2. Of those that a mesh axis runs over, the one named last changes fastest.
Arguments:
- feats: bfloat16 [256, 32768], P('rep', 'dom'), may hold values from -6 to 6
- w_self: bfloat16 [256, 256], P(None, 'rep'), may hold values from -0.375 to 0.375
- w_neigh: bfloat16 [256, 256], P(None, 'rep'), may hold values from -3 to 3
- local_cols: int32 [256, 2], P('dom'), may hold values from 0 to 31
- local_tiles: bfloat16 [256, 2, 128, 128], P('dom'), may hold values from 0 to 3, as said below
- send_list: int32 [8, 8, 2], P('dom'), may hold values from 0 to 31
- remote_rows: int32 [8, 8, 2], P('dom'), may hold values from 0 to 31
- remote_tiles: bfloat16 [8, 8, 2, 128, 128], P('dom'), may hold values from 0 to 3, as said below
- cotangent: bfloat16 [256, 32768], P('rep', 'dom'), may hold values from -6 to 6
Outputs:
- output: bfloat16 [256, 32768], P('rep', 'dom')
- grad_feats: bfloat16 [256, 32768], P('rep', 'dom')
- grad_w_self: float32 [256, 256], P(None, 'rep')
- grad_w_neigh: float32 [256, 256], P(None, 'rep')
Inputs may be any that keep to these rules, and one draw needn't show every extreme that they name: `local_tiles`: edge weights: zero where a tile has no edge, positive otherwise. `remote_tiles`: edge weights: zero where a tile has no edge, positive otherwise.
All inputs are finite; a program needn't handle non-finite values.
Results may differ from a plain program's by a relative error of at most 0.0055.
Values may be sent and summed in bfloat16 or wider, within the bound.
A program may use at most 128 MiB of HBM per device.

v0:
```python
import jax
import jax.numpy as jnp
from jax import lax
from jax.sharding import PartitionSpec as P


def local(
    feats, w_self, w_neigh, local_cols, local_tiles, send_list, remote_rows, remote_tiles, cotangent
):
    highest = lax.Precision.HIGHEST
    feat_width, node_count = feats.shape
    blocks, local_links, tile_side, _ = local_tiles.shape
    block_ids = jnp.arange(blocks, dtype=jnp.int32)
    blocked = feats.reshape(feat_width, blocks, tile_side)
    outgoing = blocked[:, send_list[0]]
    incoming = lax.all_to_all(outgoing, "dom", split_axis=1, concat_axis=1, tiled=True)
    full_feats = lax.all_gather(feats, "rep", axis=0, tiled=True)
    gathered = blocked[:, local_cols]
    summed = jnp.einsum("fblj,blij->fbi", gathered, local_tiles, preferred_element_type=jnp.float32)
    weight_rows = jnp.sum(local_tiles, axis=(1, 3), dtype=jnp.float32)
    far_tiles = remote_tiles[0]
    far_rows = remote_rows[0]
    placing = (far_rows[:, :, None] == block_ids).astype(jnp.float32)
    far_sums = jnp.sum(far_tiles, axis=3, dtype=jnp.float32)
    divisor = 1.0 + weight_rows + jnp.einsum("ski,skb->bi", far_sums, placing, precision=highest)
    far_terms = jnp.einsum(
        "fskj,skij->fski", incoming, far_tiles, preferred_element_type=jnp.float32
    )
    summed = summed + jnp.einsum("fski,skb->fbi", far_terms, placing, precision=highest)
    aggregate = (summed / divisor).astype(jnp.bfloat16).reshape(feat_width, node_count)
    full_agg = lax.all_gather(aggregate, "rep", axis=0, tiled=True)
    preact = jnp.einsum("ab,an->bn", w_self, full_feats, preferred_element_type=jnp.float32)
    preact = preact + jnp.einsum("ab,an->bn", w_neigh, full_agg, preferred_element_type=jnp.float32)
    sigmoid_val = jax.nn.sigmoid(preact)
    output = (preact * sigmoid_val).astype(jnp.bfloat16)
    slope = sigmoid_val * (1.0 + preact * (1.0 - sigmoid_val))
    grad_pre = (cotangent.astype(jnp.float32) * slope).astype(jnp.bfloat16)
    wg_self = jnp.einsum("an,bn->ab", full_feats, grad_pre, preferred_element_type=jnp.float32)
    wg_neigh = jnp.einsum("an,bn->ab", full_agg, grad_pre, preferred_element_type=jnp.float32)
    wg_self, wg_neigh = lax.psum((wg_self, wg_neigh), "dom")
    whole_self, whole_neigh = (
        lax.all_gather(w_self, "rep", axis=1, tiled=True),
        lax.all_gather(w_neigh, "rep", axis=1, tiled=True),
    )
    offset = lax.axis_index("rep") * feat_width
    mine_self = lax.dynamic_slice_in_dim(whole_self, offset, feat_width, 0)
    mine_neigh = lax.dynamic_slice_in_dim(whole_neigh, offset, feat_width, 0)
    shard_rows = lax.all_gather(grad_pre, "rep", axis=0, tiled=True)
    back_self = jnp.dot(mine_self, shard_rows, preferred_element_type=jnp.float32)
    back_agg = jnp.dot(mine_neigh, shard_rows, preferred_element_type=jnp.float32)
    scaled = (back_agg.reshape(feat_width, blocks, tile_side) / divisor).astype(jnp.bfloat16)
    picked = scaled[:, far_rows]
    far_back = jnp.einsum("fski,skij->fskj", picked, far_tiles, preferred_element_type=jnp.float32)
    returned = lax.all_to_all(far_back, "dom", split_axis=1, concat_axis=1, tiled=True)
    near_back = jnp.einsum(
        "fbi,blij->fblj", scaled, local_tiles, preferred_element_type=jnp.float32
    )
    landing = (local_cols[:, :, None] == block_ids).astype(jnp.float32)
    collected = jnp.einsum("fblj,blc->fcj", near_back, landing, precision=highest)
    homing = (send_list[0][:, :, None] == block_ids).astype(jnp.float32)
    collected = collected + jnp.einsum("fdkj,dkc->fcj", returned, homing, precision=highest)
    grad_feats = (back_self + collected.reshape(feat_width, node_count)).astype(jnp.bfloat16)
    return (output, grad_feats, wg_self, wg_neigh)


def solution(mesh):
    placed = (
        P("rep", "dom"),
        P(None, "rep"),
        P(None, "rep"),
        P("dom", None),
        P("dom", None, None, None),
        P("dom", None, None),
        P("dom", None, None),
        P("dom", None, None, None, None),
        P("rep", "dom"),
    )
    return jax.shard_map(
        local,
        mesh=mesh,
        in_specs=placed,
        out_specs=(P("rep", "dom"), P("rep", "dom"), P(None, "rep"), P(None, "rep")),
        check_vma=False,
    )
```

profile of v0, /device:TPU:0, one launch (start us, length us, event | category | flops | bytes accessed | tf_op | source)
XLA Modules:
  0.0 199.6 jit_solution(13848253110576622706)
XLA Ops:
  7.2 0.7 compare_select_fusion.1
  8.1 1.2 copy_bitcast_fusion.1
  9.3 1.3 gather_fusion.1
  10.6 7.3 %all-to-all-start = ((bf16[64,8,2,128]{3,0,2,1:T(8,128)(2,1)}), bf16[64,8,2,128]{3,0,2,1:T(8,128)(2,1)S(1)}, u32[]{:S(2)}, u32[]{:S(2)}) async-start(bf16[64,8,2,128]{3,0,2,1:T(8,128)(2,1)} %bitcast.115), calls=%async_computation | async-start | bytes 524288 | tf_op jit(solution)/shard_map/all_to_all | solution.py:16
  18.4 1.7 gather_fusion
  20.1 0.6 convert_reduce_fusion
  21.0 5.8 %all-to-all-done = bf16[64,8,2,128]{3,0,2,1:T(8,128)(2,1)S(1)} async-done(((bf16[64,8,2,128]{3,0,2,1:T(8,128)(2,1)}), bf16[64,8,2,128]{3,0,2,1:T(8,128)(2,1)S(1)}, u32[]{:S(2)}, u32[]{:S(2)}) %all-to-all-start) | async-done | bytes 262176 | tf_op jit(solution)/shard_map/all_to_all | solution.py:16
  27.3 0.9 convolution_bitcast_fusion.5
  28.2 1.1 fusion.10
  29.3 0.9 copy.71
  30.3 0.7 all-gather.4.cloned.1.call-update
  31.0 20.9 %all-gather.6.cloned.1.call-done = bf16[256,4096]{1,0:T(8,128)(2,1)} async-done(((bf16[64,4096]{1,0:T(8,128)(2,1)}), bf16[256,4096]{1,0:T(8,128)(2,1)}) %all-gather.6.cloned.1.call-update) | async-done | bytes 2097168 | tf_op jit(solution)/shard_map/all_gather | solution.py:31
  51.9 3.1 %convolution_bitcast_fusion = f32[64,4096]{1,0:T(8,128)} fusion(bf16[256,64]{0,1:T(8,128)(2,1)S(1)} %copy-done.7, bf16[256,4096]{1,0:T(8,128)(2,1)} %all-gather.6.cloned.1.call-done), kind=kOutput, calls=%fused_computation.5 | convolution fusion | flops 134217728 | bytes 3178496 | tf_op jit(solution)/shard_map/ab,an->bn/dot_general | solution.py:33
  55.0 21.1 %all-gather.4.cloned.1.call-done = bf16[256,4096]{1,0:T(8,128)(2,1)} async-done(((bf16[64,4096]{1,0:T(8,128)(2,1)}), bf16[256,4096]{1,0:T(8,128)(2,1)}) %all-gather.4.cloned.1.call-update) | async-done | bytes 2097168 | tf_op jit(solution)/shard_map/all_gather | solution.py:17
  76.1 3.6 %multiply_convert_fusion = (bf16[64,4096]{1,0:T(8,128)(2,1)}, bf16[64,4096]{1,0:T(8,128)(2,1)}) fusion(bf16[64,4096]{1,0:T(8,128)(2,1)S(1)} %copy-done.13, f32[64,4096]{1,0:T(8,128)} %convolution_bitcast_fusion, bf16[256,64]{0,1:T(8,128)(2,1)S(1)} %copy-done.8, bf16[256,4096]{1,0:T(8,128)(2,1)} %all-gather.4.cloned.1.call-done), kind=kOutput, calls=%fused_computation.28 | convolution fusion | flops 137625600 | bytes 4751360 | tf_op jit(solution)/shard_map/ab,an->bn/dot_general | solution.py:32
  79.9 5.4 %all_gather.17 = bf16[256,256]{0,1:T(8,128)(2,1)S(1)} all-gather(bf16[256,64]{0,1:T(8,128)(2,1)S(1)} %copy-done.8), channel_id=1, replica_groups=mesh['dom'=8,'rep'=4] {'rep'}, dimensions={1}, use_global_device_ids=true | all-gather | bytes 163840 | tf_op jit(solution)/shard_map/all_gather | solution.py:42
  85.3 5.6 %all_gather.19 = bf16[256,256]{0,1:T(8,128)(2,1)S(1)} all-gather(bf16[256,64]{0,1:T(8,128)(2,1)S(1)} %copy-done.7), channel_id=1, replica_groups=mesh['dom'=8,'rep'=4] {'rep'}, dimensions={1}, use_global_device_ids=true | all-gather | bytes 163840 | tf_op jit(solution)/shard_map/all_gather | solution.py:43
  91.5 11.1 %all-gather.8.cloned.1.call-done = bf16[256,4096]{1,0:T(8,128)(2,1)} async-done(((bf16[64,4096]{1,0:T(8,128)(2,1)}), bf16[256,4096]{1,0:T(8,128)(2,1)}) %all-gather.8.cloned.1.call-update) | async-done | bytes 2097168 | tf_op jit(solution)/shard_map/all_gather | solution.py:48
  102.6 2.2 %convolution_bitcast_fusion.2 = f32[8,32,8,128]{3,2,1,0:T(8,128)S(1)} fusion(bf16[256,4096]{1,0:T(8,128)(2,1)} %all-gather.8.cloned.1.call-done, bf16[256,256]{0,1:T(8,128)(2,1)S(1)} %all_gather.19, s32[]{:T(128)S(6)} %select_n.29), kind=kOutput, calls=%fused_computation.12 | convolution fusion | flops 134217728 | bytes 3211268 | tf_op jit(solution)/shard_map/dot_general | solution.py:50
  104.8 0.9 fusion.12
  105.8 1.8 gather_fusion.2
  107.5 1.1 convolution_bitcast_fusion.6
  108.6 5.5 %all-to-all-start.1 = ((f32[64,8,2,128]{3,0,2,1:T(8,128)}), f32[64,8,2,128]{3,0,2,1:T(8,128)}, u32[]{:S(2)}, u32[]{:S(2)}) async-start(f32[64,8,2,128]{3,0,2,1:T(8,128)} %convolution_bitcast_fusion.6), calls=%async_computation.1 | async-start | bytes 1048576 | tf_op jit(solution)/shard_map/all_to_all | solution.py:54
  114.2 3.1 %fusion.33 = f32[256,64]{0,1:T(8,128)} fusion(bf16[256,4096]{1,0:T(8,128)(2,1)} %all-gather.6.cloned.1.call-done, bf16[64,4096]{1,0:T(8,128)(2,1)S(1)} %copy-done.3), kind=kOutput, calls=%fused_computation.60 | convolution fusion | flops 134217728 | bytes 2686976 | tf_op jit(solution)/shard_map/an,bn->ab/dot_general | solution.py:39
  117.3 1.4 convolution_bitcast_fusion.8
  119.4 2.1 %fusion.3 = f32[32,64,128]{2,0,1:T(8,128)S(1)} fusion(f32[64,32,2,128]{3,0,2,1:T(8,128)S(1)} %convolution_bitcast_fusion.1, s32[32,2]{0,1:T(2,128)S(1)} %copy-done.10), kind=kOutput, calls=%fused_computation.11 | convolution fusion | flops 201328640 | bytes 3145984 | tf_op jit(solution)/shard_map/fblj,blc->fcj/dot_general | solution.py:59
  121.5 8.1 %all-to-all-done.1 = f32[64,8,2,128]{3,0,2,1:T(8,128)} async-done(((f32[64,8,2,128]{3,0,2,1:T(8,128)}), f32[64,8,2,128]{3,0,2,1:T(8,128)}, u32[]{:S(2)}, u32[]{:S(2)}) %all-to-all-start.1) | async-done | bytes 524320 | tf_op jit(solution)/shard_map/all_to_all | solution.py:54
  129.6 1.9 fusion.8
  131.5 1.8 fusion
  133.3 56.8 %all-reduce.3.cloned.1.call-done = (f32[256,64]{0,1:T(8,128)}, f32[256,64]{0,1:T(8,128)}) async-done(((f32[256,64]{0,1:T(8,128)}, f32[256,64]{0,1:T(8,128)}), (f32[256,64]{0,1:T(8,128)}, f32[256,64]{0,1:T(8,128)})) %all-reduce.3.cloned.1.call-update) | async-done | bytes 131088 | tf_op jit(solution)/shard_map/psum | solution.py:40
  190.1 1.5 copy.74
  191.6 1.5 copy.75
  (50 shorter events, 3.0 us)
Async XLA Ops:
  7.2 10.8 %copy-start.9 = (s32[32,2]{0,1:T(2,128)S(1)}, s32[32,2]{0,1:T(2,128)}, u32[]{:S(2)}) copy-start(s32[32,2]{0,1:T(2,128)} %param.12) | copy-start | bytes 772
  7.2 10.8 %copy-start.2 = (bf16[1,8,2,128,128]{4,3,2,1,0:T(8,128)(2,1)S(1)}, bf16[1,8,2,128,128]{4,3,2,1,0:T(8,128)(2,1)}, u32[]{:S(2)}) copy-start(bf16[1,8,2,128,128]{4,3,2,1,0:T(8,128)(2,1)} %param.16) | copy-start | bytes 1572868
  9.3 10.8 %copy-start = (bf16[32,2,128,128]{3,2,1,0:T(8,128)(2,1)S(1)}, bf16[32,2,128,128]{3,2,1,0:T(8,128)(2,1)}, u32[]{:S(2)}) copy-start(bf16[32,2,128,128]{3,2,1,0:T(8,128)(2,1)} %param.13) | copy-start | bytes 6291460
  10.6 16.2 %all-to-all-start = ((bf16[64,8,2,128]{3,0,2,1:T(8,128)(2,1)}), bf16[64,8,2,128]{3,0,2,1:T(8,128)(2,1)S(1)}, u32[]{:S(2)}, u32[]{:S(2)}) async-start(bf16[64,8,2,128]{3,0,2,1:T(8,128)(2,1)} %bitcast.115), calls=%async_computation | async-start | bytes 524288 | tf_op jit(solution)/shard_map/all_to_all | solution.py:16
  17.9 34.1 %all-gather.6.cloned.1.call-start = ((), (), s32[]{:S(2)}) async-start(), calls=%async_computation.3 | async-start | bytes 2621440 | tf_op jit(solution)/shard_map/all_gather | solution.py:31
  18.4 2.3 %copy-start.12 = (s32[1,8,2]{1,2,0:T(2,128)S(1)}, s32[1,8,2]{1,2,0:T(2,128)}, u32[]{:S(2)}) copy-start(s32[1,8,2]{1,2,0:T(2,128)} %param.15) | copy-start | bytes 196
  26.8 1.4 copy-start.6
  29.3 22.6 %copy-start.7 = (bf16[256,64]{0,1:T(8,128)(2,1)S(1)}, bf16[256,64]{0,1:T(8,128)(2,1)}, u32[]{:S(2)}) copy-start(bf16[256,64]{0,1:T(8,128)(2,1)} %param.11) | copy-start | bytes 98308
  30.2 45.9 %copy-start.8 = (bf16[256,64]{0,1:T(8,128)(2,1)S(1)}, bf16[256,64]{0,1:T(8,128)(2,1)}, u32[]{:S(2)}) copy-start(bf16[256,64]{0,1:T(8,128)(2,1)} %param.10) | copy-start | bytes 98308
  30.2 45.9 %copy-start.13 = (bf16[64,4096]{1,0:T(8,128)(2,1)S(1)}, bf16[64,4096]{1,0:T(8,128)(2,1)}, u32[]{:S(2)}) copy-start(bf16[64,4096]{1,0:T(8,128)(2,1)} %param.17) | copy-start | bytes 1572868
  30.2 45.9 %all-gather.4.cloned.1.call-start = ((), (), s32[]{:S(2)}) async-start(), calls=%async_computation.2 | async-start | bytes 2621440 | tf_op jit(solution)/shard_map/all_gather | solution.py:17
  31.0 71.7 %all-gather.8.cloned.1.call-start = ((), (), s32[]{:S(2)}) async-start(), calls=%async_computation.4 | async-start | bytes 2621440 | tf_op jit(solution)/shard_map/all_gather | solution.py:48
  104.8 9.3 %copy-start.3 = (bf16[64,4096]{1,0:T(8,128)(2,1)S(1)}, bf16[64,4096]{1,0:T(8,128)(2,1)}, u32[]{:S(2)}) copy-start(bf16[64,4096]{1,0:T(8,128)(2,1)} %get-tuple-element.6) | copy-start | bytes 1572868
  108.6 21.0 %all-to-all-start.1 = ((f32[64,8,2,128]{3,0,2,1:T(8,128)}), f32[64,8,2,128]{3,0,2,1:T(8,128)}, u32[]{:S(2)}, u32[]{:S(2)}) async-start(f32[64,8,2,128]{3,0,2,1:T(8,128)} %convolution_bitcast_fusion.6), calls=%async_computation.1 | async-start | bytes 1048576 | tf_op jit(solution)/shard_map/all_to_all | solution.py:54
  114.1 4.6 %copy-start.4 = (bf16[64,32,128]{2,0,1:T(8,128)(2,1)S(1)}, bf16[64,32,128]{2,0,1:T(8,128)(2,1)}, u32[]{:S(2)}) copy-start(bf16[64,32,128]{2,0,1:T(8,128)(2,1)} %fusion.12) | copy-start | bytes 1572868
  114.1 76.0 %all-reduce.3.cloned.1.call-start = ((), (), s32[]{:S(2)}) async-start(), calls=%async_computation.5 | async-start | bytes 262144 | tf_op jit(solution)/shard_map/psum | solution.py:40
  114.2 3.1 %copy-start.5 = (bf16[256,4096]{1,0:T(8,128)(2,1)S(1)}, bf16[256,4096]{1,0:T(8,128)(2,1)}, u32[]{:S(2)}) copy-start(bf16[256,4096]{1,0:T(8,128)(2,1)} %all-gather.4.cloned.1.call-done) | copy-start | bytes 6291460
  118.7 0.7 copy-start.10
  119.4 10.2 %copy-start.11 = (s32[1,8,2]{1,2,0:T(2,128)S(1)}, s32[1,8,2]{1,2,0:T(2,128)}, u32[]{:S(2)}) copy-start(s32[1,8,2]{1,2,0:T(2,128)} %param.14) | copy-start | bytes 196
  121.5 10.0 %copy-start.1 = (bf16[256,4096]{1,0:T(8,128)(2,1)S(1)}, bf16[256,4096]{1,0:T(8,128)(2,1)}, u32[]{:S(2)}) copy-start(bf16[256,4096]{1,0:T(8,128)(2,1)} %all-gather.8.cloned.1.call-done) | copy-start | bytes 6291460
Sparse Core Ops, SparseCore 0:
  30.3 21.5 all-gather.5
  53.5 22.5 all-gather.3
  79.8 22.7 all-gather.7
  118.9 71.2 all-reduce.2
where the time goes:
time: 200 us
  waiting for transfers between devices  125 us (62%)
  matrix products  23.3 us (12%)
  between operations  14 us (7%)
  starting transfers between devices  13 us (6%)
  blocking collectives  11 us (6%)
  local copies, waits for them, and re-layouts  10.5 us (5%)
  other arithmetic  3.12 us (2%)
    psum x1, waiting for transfers between devices, local(): wg_self, wg_neigh = lax.psum((wg_self, wg_neigh), 'dom')  56.8 us
    all_gather x1, waiting for transfers between devices, local(): full_feats = lax.all_gather(feats, 'rep', axis=0, tiled=True)  21.1 us
    all_gather x1, waiting for transfers between devices, local(): full_agg = lax.all_gather(aggregate, 'rep', axis=0, tiled=True)  20.9 us
    all_gather x1, waiting for transfers between devices, local(): shard_rows = lax.all_gather(grad_pre, 'rep', axis=0, tiled=True)  11.1 us
    all_to_all x1, waiting for transfers between devices, local(): lax.all_to_all(far_back, 'dom', split_axis=1, concat_axis=1, tiled=True)  8.12 us
    all_to_all x1, starting transfers between devices, local(): lax.all_to_all(outgoing, 'dom', split_axis=1, concat_axis=1, tiled=True)  7.31 us
    all_to_all x1, waiting for transfers between devices, local(): lax.all_to_all(outgoing, 'dom', split_axis=1, concat_axis=1, tiled=True)  5.82 us
    all_gather x1, blocking collectives, local(): lax.all_gather(w_neigh, 'rep', axis=1, tiled=True)  5.6 us
  transfers between devices with their start and end apart: 6, of which 6 were waited for; matrix products, arithmetic and copies ran while one was open for 9% of the time, Pallas kernels for 0%

commit v1 on v0

--- a/solution.py
+++ b/solution.py
@@ -14,7 +14,12 @@
     blocked = feats.reshape(feat_width, blocks, tile_side)
     outgoing = blocked[:, send_list[0]]
     incoming = lax.all_to_all(outgoing, "dom", split_axis=1, concat_axis=1, tiled=True)
-    full_feats = lax.all_gather(feats, "rep", axis=0, tiled=True)
+    ring = [feats]
+    for hop in range(3):
+        ring.append(lax.ppermute(ring[-1], "rep", [(dev, (dev + 1) % 4) for dev in range(4)]))
+    full_feats = jnp.roll(
+        jnp.concatenate(ring[::-1], axis=0), (lax.axis_index("rep") + 1) * ring[0].shape[0], axis=0
+    )
     gathered = blocked[:, local_cols]
     summed = jnp.einsum("fblj,blij->fbi", gathered, local_tiles, preferred_element_type=jnp.float32)
     weight_rows = jnp.sum(local_tiles, axis=(1, 3), dtype=jnp.float32)

time: 200 us -> 182 us (0.910)
  waiting for transfers between devices: 125 us -> 92.3 us
  local copies, waits for them, and re-layouts: 10.5 us -> 23.6 us
    all_gather x1 -> x0, waiting for transfers between devices: 21.1 us -> none  [local(): full_feats = lax.all_gather(feats, 'rep', axis=0, tiled=True)]
    all_gather x1, waiting for transfers between devices: 20.9 us -> 5.85 us  [local(): full_agg = lax.all_gather(aggregate, 'rep', axis=0, tiled=True)]
    unnamed x30 -> x39, local copies, waits for them, and re-layouts: 3.23 us -> 15.4 us
    ppermute x0 -> x3, waiting for transfers between devices: none -> 10 us  [local(): lax.ppermute(ring[-1], 'rep', [(dev, (dev + 1) % 4) for dev in range(4)])]
    all_to_all x1, waiting for transfers between devices: 5.82 us -> 0.48 us  [local(): lax.all_to_all(outgoing, 'dom', split_axis=1, concat_axis=1, tiled=True)]
  transfers between devices with their start and end apart: 6 -> 8, of which waited for: 6 -> 7; matrix products, arithmetic and copies ran while one was open for 9% -> 19% of each run, Pallas kernels for 0% -> 0%
where the time goes in v1:
time: 182 us; the launch traced here: 181 us
  waiting for transfers between devices  92.3 us (51%)
  local copies, waits for them, and re-layouts  23.6 us (13%)
  matrix products  22.1 us (12%)
  starting transfers between devices  14.6 us (8%)
  between operations  14 us (8%)
  blocking collectives  11 us (6%)
  other arithmetic  3.24 us (2%)
    psum x1, waiting for transfers between devices, local(): wg_self, wg_neigh = lax.psum((wg_self, wg_neigh), 'dom')  56.9 us
    unnamed x39, local copies, waits for them, and re-layouts  15.4 us
    all_gather x1, waiting for transfers between devices, local(): shard_rows = lax.all_gather(grad_pre, 'rep', axis=0, tiled=True)  11.2 us
    ppermute x3, waiting for transfers between devices, local(): lax.ppermute(ring[-1], 'rep', [(dev, (dev + 1) % 4) for dev in range(4)])  10 us
    all_to_all x1, waiting for transfers between devices, local(): lax.all_to_all(far_back, 'dom', split_axis=1, concat_axis=1, tiled=True)  7.93 us
    all_to_all x1, starting transfers between devices, local(): lax.all_to_all(outgoing, 'dom', split_axis=1, concat_axis=1, tiled=True)  6.88 us
    all_gather x1, waiting for transfers between devices, local(): full_agg = lax.all_gather(aggregate, 'rep', axis=0, tiled=True)  5.85 us
    all_gather x1, blocking collectives, local(): lax.all_gather(w_self, 'rep', axis=1, tiled=True)  5.59 us
  transfers between devices with their start and end apart: 8, of which 7 were waited for; matrix products, arithmetic and copies ran while one was open for 19% of the time, Pallas kernels for 0%

profile of v1, /device:TPU:0, one launch (start us, length us, event | category | flops | bytes accessed | tf_op | source)
XLA Modules:
  0.0 180.8 jit_solution(13490284826771740564)
XLA Ops:
  7.7 1.2 copy_bitcast_fusion.1
  9.9 1.3 gather_fusion.1
  11.2 6.9 %all-to-all-start = ((bf16[64,8,2,128]{3,0,2,1:T(8,128)(2,1)}), bf16[64,8,2,128]{3,0,2,1:T(8,128)(2,1)S(1)}, u32[]{:S(2)}, u32[]{:S(2)}) async-start(bf16[64,8,2,128]{3,0,2,1:T(8,128)(2,1)} %bitcast.111), calls=%async_computation | async-start | bytes 524288 | tf_op jit(solution)/shard_map/all_to_all | solution.py:16
  18.6 1.3 collective-permute-start.1
  20.0 1.7 gather_fusion
  22.6 5.0 %collective-permute-done.1 = bf16[64,4096]{1,0:T(8,128)(2,1)} collective-permute-done((bf16[64,4096]{1,0:T(8,128)(2,1)}, bf16[64,4096]{1,0:T(8,128)(2,1)}, u32[]{:S(2)}, u32[]{:S(2)}) %collective-permute-start.1) | collective-permute-done | bytes 524320 | tf_op jit(solution)/shard_map/ppermute | solution.py:19
  29.4 1.1 fusion.14
  31.5 5.0 %collective-permute-done.2 = bf16[64,4096]{1,0:T(8,128)(2,1)} collective-permute-done((bf16[64,4096]{1,0:T(8,128)(2,1)}, bf16[64,4096]{1,0:T(8,128)(2,1)}, u32[]{:S(2)}, u32[]{:S(2)}) %collective-permute-start.2) | collective-permute-done | bytes 524320 | tf_op jit(solution)/shard_map/ppermute | solution.py:19
  36.5 1.9 %constant_dynamic-update-slice_fusion.7 = bf16[512,4096]{1,0:T(8,128)(2,1)} fusion(bf16[64,4096]{1,0:T(8,128)(2,1)} %collective-permute-done.2), kind=kLoop, calls=%fused_computation.52 | loop fusion | bytes 1048576
  38.4 1.9 %constant_dynamic-update-slice_fusion.6 = bf16[512,4096]{1,0:T(8,128)(2,1)} fusion(bf16[512,4096]{1,0:T(8,128)(2,1)} %constant_dynamic-update-slice_fusion.7, bf16[64,4096]{1,0:T(8,128)(2,1)} %collective-permute-done.1), kind=kLoop, calls=%fused_computation.51 | loop fusion | bytes 1048576
  40.3 2.0 %constant_dynamic-update-slice_fusion.5 = bf16[512,4096]{1,0:T(8,128)(2,1)} fusion(bf16[512,4096]{1,0:T(8,128)(2,1)} %constant_dynamic-update-slice_fusion.6, bf16[64,4096]{1,0:T(8,128)(2,1)} %collective-permute-done), kind=kLoop, calls=%fused_computation.50 | loop fusion | bytes 1048576
  43.1 1.9 %constant_dynamic-update-slice_fusion.3 = bf16[512,4096]{1,0:T(8,128)(2,1)} fusion(bf16[512,4096]{1,0:T(8,128)(2,1)} %constant_dynamic-update-slice_fusion.4, bf16[64,4096]{1,0:T(8,128)(2,1)} %collective-permute-done.2), kind=kLoop, calls=%fused_computation.48 | loop fusion | bytes 1048576
  45.0 1.9 %constant_dynamic-update-slice_fusion.2 = bf16[512,4096]{1,0:T(8,128)(2,1)} fusion(bf16[512,4096]{1,0:T(8,128)(2,1)} %constant_dynamic-update-slice_fusion.3, bf16[64,4096]{1,0:T(8,128)(2,1)} %collective-permute-done.1), kind=kLoop, calls=%fused_computation.47 | loop fusion | bytes 1048576
  46.9 1.9 %constant_dynamic-update-slice_fusion.1 = bf16[512,4096]{1,0:T(8,128)(2,1)} fusion(bf16[512,4096]{1,0:T(8,128)(2,1)} %constant_dynamic-update-slice_fusion.2, bf16[64,4096]{1,0:T(8,128)(2,1)} %collective-permute-done), kind=kLoop, calls=%fused_computation.46 | loop fusion | bytes 1048576
  49.5 5.9 %all-gather.3.cloned.1.call-done = bf16[256,4096]{1,0:T(8,128)(2,1)} async-done(((bf16[64,4096]{1,0:T(8,128)(2,1)}), bf16[256,4096]{1,0:T(8,128)(2,1)}) %all-gather.3.cloned.1.call-update) | async-done | bytes 2097168 | tf_op jit(solution)/shard_map/all_gather | solution.py:36
  55.4 2.1 %fusion.40 = f32[4096,64]{0,1:T(8,128)S(1)} fusion(bf16[256,64]{0,1:T(8,128)(2,1)S(1)} %copy-done.8, bf16[256,4096]{1,0:T(8,128)(2,1)} %all-gather.3.cloned.1.call-done), kind=kOutput, calls=%fused_computation.73 | convolution fusion | flops 134217728 | bytes 3178496 | tf_op jit(solution)/shard_map/ab,an->bn/dot_general | solution.py:38
  57.5 3.4 %multiply_convert_fusion = (bf16[64,4096]{1,0:T(8,128)(2,1)}, bf16[64,4096]{1,0:T(8,128)(2,1)}) fusion(bf16[64,4096]{1,0:T(8,128)(2,1)S(1)} %copy-done.14, f32[4096,64]{0,1:T(8,128)S(1)} %fusion.40, bf16[256,64]{0,1:T(8,128)(2,1)S(1)} %copy-done.9, bf16[512,4096]{1,0:T(8,128)(2,1)} %constant_dynamic-update-slice_fusion, s32[]{:T(128)S(6)} %select_n.41), kind=kOutput, calls=%fused_computation.30 | convolution fusion | flops 137625600 | bytes 4751364 | tf_op jit(solution)/shard_map/ab,an->bn/dot_general | solution.py:37
  61.0 5.4 %all_gather.15 = bf16[256,256]{0,1:T(8,128)(2,1)S(1)} all-gather(bf16[256,64]{0,1:T(8,128)(2,1)S(1)} %copy-done.8), channel_id=1, replica_groups=mesh['dom'=8,'rep'=4] {'rep'}, dimensions={1}, use_global_device_ids=true | all-gather | bytes 163840 | tf_op jit(solution)/shard_map/all_gather | solution.py:48
  66.4 5.6 %all_gather.13 = bf16[256,256]{0,1:T(8,128)(2,1)S(1)} all-gather(bf16[256,64]{0,1:T(8,128)(2,1)S(1)} %copy-done.9), channel_id=1, replica_groups=mesh['dom'=8,'rep'=4] {'rep'}, dimensions={1}, use_global_device_ids=true | all-gather | bytes 163840 | tf_op jit(solution)/shard_map/all_gather | solution.py:47
  72.6 11.2 %all-gather.5.cloned.1.call-done = bf16[256,4096]{1,0:T(8,128)(2,1)} async-done(((bf16[64,4096]{1,0:T(8,128)(2,1)}), bf16[256,4096]{1,0:T(8,128)(2,1)}) %all-gather.5.cloned.1.call-update) | async-done | bytes 2097168 | tf_op jit(solution)/shard_map/all_gather | solution.py:53
  83.8 2.2 %convolution_bitcast_fusion.1 = f32[8,32,8,128]{3,2,1,0:T(8,128)S(1)} fusion(bf16[256,4096]{1,0:T(8,128)(2,1)} %all-gather.5.cloned.1.call-done, bf16[256,256]{0,1:T(8,128)(2,1)S(1)} %all_gather.15, s32[]{:T(128)S(6)} %select_n.44), kind=kOutput, calls=%fused_computation.15 | convolution fusion | flops 134217728 | bytes 3211268 | tf_op jit(solution)/shard_map/dot_general | solution.py:55
  86.9 1.8 gather_fusion.2
  89.7 5.5 %all-to-all-start.1 = ((f32[64,8,2,128]{3,0,2,1:T(8,128)}), f32[64,8,2,128]{3,0,2,1:T(8,128)}, u32[]{:S(2)}, u32[]{:S(2)}) async-start(f32[64,8,2,128]{3,0,2,1:T(8,128)} %convolution_bitcast_fusion.5), calls=%async_computation.1 | async-start | bytes 1048576 | tf_op jit(solution)/shard_map/all_to_all | solution.py:59
  95.5 3.1 %fusion.4 = f32[256,64]{0,1:T(8,128)} fusion(bf16[64,4096]{1,0:T(8,128)(2,1)S(1)} %copy-done.5, bf16[512,4096]{1,0:T(8,128)(2,1)} %constant_dynamic-update-slice_fusion, s32[]{:T(128)S(6)} %select_n.41), kind=kOutput, calls=%fused_computation.10 | convolution fusion | flops 134217728 | bytes 2686980 | tf_op jit(solution)/shard_map/an,bn->ab/dot_general | solution.py:43
  98.7 1.4 fusion.39
  100.8 2.1 %fusion.7 = f32[32,64,128]{2,0,1:T(8,128)S(1)} fusion(f32[64,32,2,128]{3,0,2,1:T(8,128)S(1)} %convolution_bitcast_fusion, s32[32,2]{0,1:T(2,128)S(1)} %copy-done.11), kind=kOutput, calls=%fused_computation.14 | convolution fusion | flops 201328640 | bytes 3145984 | tf_op jit(solution)/shard_map/fblj,blc->fcj/dot_general | solution.py:64
  102.8 7.9 %all-to-all-done.1 = f32[64,8,2,128]{3,0,2,1:T(8,128)} async-done(((f32[64,8,2,128]{3,0,2,1:T(8,128)}), f32[64,8,2,128]{3,0,2,1:T(8,128)}, u32[]{:S(2)}, u32[]{:S(2)}) %all-to-all-start.1) | async-done | bytes 524320 | tf_op jit(solution)/shard_map/all_to_all | solution.py:59
  110.8 1.9 %fusion.12 = f32[32,64,128]{2,0,1:T(8,128)S(1)} fusion(f32[32,64,128]{2,0,1:T(8,128)S(1)} %fusion.7, f32[64,8,2,128]{3,0,2,1:T(8,128)} %all-to-all-done.1, s32[8,2]{0,1:T(2,128)S(1)} %bitcast.112), kind=kOutput, calls=%fused_computation.21 | convolution fusion | flops 50594304 | bytes 2621504 | tf_op jit(solution)/shard_map/fdkj,dkc->fcj/dot_general | solution.py:66
  112.7 1.8 fusion.1
  114.5 56.9 %all-reduce.3.cloned.1.call-done = (f32[256,64]{0,1:T(8,128)}, f32[256,64]{0,1:T(8,128)}) async-done(((f32[256,64]{0,1:T(8,128)}, f32[256,64]{0,1:T(8,128)}), (f32[256,64]{0,1:T(8,128)}, f32[256,64]{0,1:T(8,128)})) %all-reduce.3.cloned.1.call-update) | async-done | bytes 131088 | tf_op jit(solution)/shard_map/psum | solution.py:45
  171.4 1.5 copy.81
  172.8 1.5 copy.82
  (62 shorter events, 11.1 us)
Async XLA Ops:
  7.2 11.0 %copy-start.10 = (s32[32,2]{0,1:T(2,128)S(1)}, s32[32,2]{0,1:T(2,128)}, u32[]{:S(2)}) copy-start(s32[32,2]{0,1:T(2,128)} %param.12) | copy-start | bytes 772
  7.2 11.2 %copy-start.4 = (bf16[1,8,2,128,128]{4,3,2,1,0:T(8,128)(2,1)S(1)}, bf16[1,8,2,128,128]{4,3,2,1,0:T(8,128)(2,1)}, u32[]{:S(2)}) copy-start(bf16[1,8,2,128,128]{4,3,2,1,0:T(8,128)(2,1)} %param.16) | copy-start | bytes 1572868
  7.2 11.4 %collective-permute-start = (bf16[64,4096]{1,0:T(8,128)(2,1)}, bf16[64,4096]{1,0:T(8,128)(2,1)}, u32[]{:S(2)}, u32[]{:S(2)}) collective-permute-start(bf16[64,4096]{1,0:T(8,128)(2,1)} %param.9), channel_id=1, source_target_pairs={{0,1},{1,2},{2,3},{3,0},{4,5},{5,6},{6,7},{7,4},{8,9},{9,10},{10,1... | collective-permute-start | bytes 1572872 | tf_op jit(solution)/shard_map/ppermute | solution.py:19
  8.9 12.8 %copy-start = (bf16[32,2,128,128]{3,2,1,0:T(8,128)(2,1)S(1)}, bf16[32,2,128,128]{3,2,1,0:T(8,128)(2,1)}, u32[]{:S(2)}) copy-start(bf16[32,2,128,128]{3,2,1,0:T(8,128)(2,1)} %param.13) | copy-start | bytes 6291460
  11.2 16.8 %all-to-all-start = ((bf16[64,8,2,128]{3,0,2,1:T(8,128)(2,1)}), bf16[64,8,2,128]{3,0,2,1:T(8,128)(2,1)S(1)}, u32[]{:S(2)}, u32[]{:S(2)}) async-start(bf16[64,8,2,128]{3,0,2,1:T(8,128)(2,1)} %bitcast.111), calls=%async_computation | async-start | bytes 524288 | tf_op jit(solution)/shard_map/all_to_all | solution.py:16
  18.1 37.3 %all-gather.3.cloned.1.call-start = ((), (), s32[]{:S(2)}) async-start(), calls=%async_computation.2 | async-start | bytes 2621440 | tf_op jit(solution)/shard_map/all_gather | solution.py:36
  18.6 9.0 %collective-permute-start.1 = (bf16[64,4096]{1,0:T(8,128)(2,1)}, bf16[64,4096]{1,0:T(8,128)(2,1)}, u32[]{:S(2)}, u32[]{:S(2)}) collective-permute-start(bf16[64,4096]{1,0:T(8,128)(2,1)} %collective-permute-done), channel_id=1, source_target_pairs={{0,1},{1,2},{2,3},{3,0},{4,5},{5,6},{6,7},{7,4},{8,9},{9,10},{10,1... | collective-permute-start | bytes 1572872 | tf_op jit(solution)/shard_map/ppermute | solution.py:19
  20.0 2.3 %copy-start.13 = (s32[1,8,2]{1,2,0:T(2,128)S(1)}, s32[1,8,2]{1,2,0:T(2,128)}, u32[]{:S(2)}) copy-start(s32[1,8,2]{1,2,0:T(2,128)} %param.15) | copy-start | bytes 196
  27.6 8.9 %collective-permute-start.2 = (bf16[64,4096]{1,0:T(8,128)(2,1)}, bf16[64,4096]{1,0:T(8,128)(2,1)}, u32[]{:S(2)}, u32[]{:S(2)}) collective-permute-start(bf16[64,4096]{1,0:T(8,128)(2,1)} %collective-permute-done.1), channel_id=1, source_target_pairs={{0,1},{1,2},{2,3},{3,0},{4,5},{5,6},{6,7},{7,4},{8,9},{9,10},{10,1... | collective-permute-start | bytes 1572872 | tf_op jit(solution)/shard_map/ppermute | solution.py:19
  28.1 1.4 copy-start.7
  31.4 10.8 %copy-start.3 = (bf16[64,4096]{1,0:T(8,128)(2,1)S(1)}, bf16[64,4096]{1,0:T(8,128)(2,1)}, u32[]{:S(2)}) copy-start(bf16[64,4096]{1,0:T(8,128)(2,1)} %param.9) | copy-start | bytes 1572868
  31.5 52.3 %all-gather.5.cloned.1.call-start = ((), (), s32[]{:S(2)}) async-start(), calls=%async_computation.3 | async-start | bytes 2621440 | tf_op jit(solution)/shard_map/all_gather | solution.py:53
  43.1 12.3 %copy-start.8 = (bf16[256,64]{0,1:T(8,128)(2,1)S(1)}, bf16[256,64]{0,1:T(8,128)(2,1)}, u32[]{:S(2)}) copy-start(bf16[256,64]{0,1:T(8,128)(2,1)} %param.11) | copy-start | bytes 98308
  48.7 8.7 %copy-start.9 = (bf16[256,64]{0,1:T(8,128)(2,1)S(1)}, bf16[256,64]{0,1:T(8,128)(2,1)}, u32[]{:S(2)}) copy-start(bf16[256,64]{0,1:T(8,128)(2,1)} %param.10) | copy-start | bytes 98308
  49.5 7.9 %copy-start.14 = (bf16[64,4096]{1,0:T(8,128)(2,1)S(1)}, bf16[64,4096]{1,0:T(8,128)(2,1)}, u32[]{:S(2)}) copy-start(bf16[64,4096]{1,0:T(8,128)(2,1)} %param.17) | copy-start | bytes 1572868
  86.0 9.5 %copy-start.5 = (bf16[64,4096]{1,0:T(8,128)(2,1)S(1)}, bf16[64,4096]{1,0:T(8,128)(2,1)}, u32[]{:S(2)}) copy-start(bf16[64,4096]{1,0:T(8,128)(2,1)} %get-tuple-element.6) | copy-start | bytes 1572868
  89.7 21.0 %all-to-all-start.1 = ((f32[64,8,2,128]{3,0,2,1:T(8,128)}), f32[64,8,2,128]{3,0,2,1:T(8,128)}, u32[]{:S(2)}, u32[]{:S(2)}) async-start(f32[64,8,2,128]{3,0,2,1:T(8,128)} %convolution_bitcast_fusion.5), calls=%async_computation.1 | async-start | bytes 1048576 | tf_op jit(solution)/shard_map/all_to_all | solution.py:59
  95.3 4.8 %copy-start.6 = (bf16[64,32,128]{2,0,1:T(8,128)(2,1)S(1)}, bf16[64,32,128]{2,0,1:T(8,128)(2,1)}, u32[]{:S(2)}) copy-start(bf16[64,32,128]{2,0,1:T(8,128)(2,1)} %fusion.16) | copy-start | bytes 1572868
  95.3 76.1 %all-reduce.3.cloned.1.call-start = ((), (), s32[]{:S(2)}) async-start(), calls=%async_computation.4 | async-start | bytes 262144 | tf_op jit(solution)/shard_map/psum | solution.py:45
  95.5 3.1 %copy-start.1 = (bf16[256,4096]{1,0:T(8,128)(2,1)S(1)}, bf16[256,4096]{1,0:T(8,128)(2,1)}, u32[]{:S(2)}) copy-start(bf16[256,4096]{1,0:T(8,128)(2,1)} %all-gather.3.cloned.1.call-done) | copy-start | bytes 6291460
  100.1 0.7 copy-start.11
  100.8 10.0 %copy-start.12 = (s32[1,8,2]{1,2,0:T(2,128)S(1)}, s32[1,8,2]{1,2,0:T(2,128)}, u32[]{:S(2)}) copy-start(s32[1,8,2]{1,2,0:T(2,128)} %param.14) | copy-start | bytes 196
  102.8 9.9 %copy-start.2 = (bf16[256,4096]{1,0:T(8,128)(2,1)S(1)}, bf16[256,4096]{1,0:T(8,128)(2,1)}, u32[]{:S(2)}) copy-start(bf16[256,4096]{1,0:T(8,128)(2,1)} %all-gather.5.cloned.1.call-done) | copy-start | bytes 6291460
Sparse Core Ops, SparseCore 0:
  31.6 23.7 all-gather.2
  61.0 22.7 all-gather.4
  100.2 71.1 all-reduce.2
